TPU v7x, 32 devices: a whole 2x2x4 slice. The times are simulated.
32 devices in a mesh: fsdp: 4 (over y, x), context: 4 (over z), tensor: 2 (over core).
Axes of the slice: x: 2, y: 2, z: 4, core: 2. Of those that a mesh axis runs over, the one named last changes fastest.
Arguments:
- layer_input: bfloat16 [4, 1024, 2048], P('fsdp', 'context'), may hold values from -6 to 6
- prefix: int32 [4], P('fsdp'), may hold values from 102 to 512
- attn_gain: float32 [2048], P(('fsdp', 'context')), may hold values from 0.1 to 1.9
- q_weight: float32 [2048, 2048], P(('fsdp', 'context'), 'tensor'), may hold values from -0.125 to 0.125
- k_weight: float32 [2048, 512], P(('fsdp', 'context'), 'tensor'), may hold values from -0.125 to 0.125
- v_weight: float32 [2048, 512], P(('fsdp', 'context'), 'tensor'), may hold values from -0.125 to 0.125
- output_weight: float32 [2048, 2048], P(('fsdp', 'context'), 'tensor'), may hold values from -0.75 to 0.75
- mlp_gain: float32 [2048], P(('fsdp', 'context')), may hold values from 0.1 to 1.9
- gate_weight: float32 [2048, 8192], P(('fsdp', 'context'), 'tensor'), may hold values from -0.125 to 0.125
- up_weight: float32 [2048, 8192], P(('fsdp', 'context'), 'tensor'), may hold values from -0.125 to 0.125
- down_weight: float32 [2048, 8192], P(('fsdp', 'context'), 'tensor'), may hold values from -0.0625 to 0.0625
- cotangent: bfloat16 [4, 1024, 2048], P('fsdp', 'context'), may hold values from -6 to 6
Outputs:
- layer_output: bfloat16 [4, 1024, 2048], P('fsdp', 'context')
- input_grad: bfloat16 [4, 1024, 2048], P('fsdp', 'context')
- attn_gain_grad: float32 [2048], P(('fsdp', 'context'))
- q_weight_grad: float32 [2048, 2048], P(('fsdp', 'context'), 'tensor')
- k_weight_grad: float32 [2048, 512], P(('fsdp', 'context'), 'tensor')
- v_weight_grad: float32 [2048, 512], P(('fsdp', 'context'), 'tensor')
- o_weight_grad: float32 [2048, 2048], P(('fsdp', 'context'), 'tensor')
- mlp_gain_grad: float32 [2048], P(('fsdp', 'context'))
- gate_weight_grad: float32 [2048, 8192], P(('fsdp', 'context'), 'tensor')
- up_weight_grad: float32 [2048, 8192], P(('fsdp', 'context'), 'tensor')
- down_weight_grad: float32 [2048, 8192], P(('fsdp', 'context'), 'tensor')
Inputs may be any that keep to these rules, and one draw needn't show every extreme that they name: prefix counts whole leading tokens of a sequence of 1024.
All inputs are finite; a program needn't handle non-finite values.
Results may differ from a plain program's by a relative error of at most 0.019.
Values may be sent and summed in bfloat16 or wider, within the bound.
No kernel may reach another device: no remote copies, remote signals or barrier semaphores. Data moves between devices by JAX's collectives and lax.ppermute only.
A program may use at most 384 MiB of HBM per device.

v0:
```python
from functools import partial
import math
import jax
import jax.numpy as jnp
from jax import lax
from jax.sharding import PartitionSpec as P

HEADS = 32
KV_HEADS = 8
HEAD_DIM = 64
EPS = 1e-05


def rope_tables(length, head_dim):
    half_dim = head_dim // 2
    freq_index = jnp.arange(half_dim, dtype=jnp.float32)
    base_freq = 1.0 / jnp.power(500000.0, 2.0 * freq_index / head_dim)
    wave_len = 2.0 * math.pi / base_freq
    mix_ratio = jnp.clip((8192.0 / wave_len - 1.0) / 3.0, 0.0, 1.0)
    scaled = (1.0 - mix_ratio) * base_freq / 32.0 + mix_ratio * base_freq
    position = jnp.arange(length, dtype=jnp.float32)
    angles = position[:, None] * scaled[None, :]
    angles = jnp.concatenate([angles, angles], axis=1)
    return (jnp.cos(angles), jnp.sin(angles))


def rotate(tensor_in, cos_table, sin_table):
    half_dim = tensor_in.shape[-1] // 2
    turned = jnp.concatenate([-tensor_in[..., half_dim:], tensor_in[..., :half_dim]], axis=-1)
    return tensor_in * cos_table[:, None, :] + turned * sin_table[:, None, :]


def rotate_rows(flat_in, cos_table, sin_table):
    shaped = flat_in.reshape(flat_in.shape[0], flat_in.shape[1], -1, HEAD_DIM)
    return rotate(shaped, cos_table, sin_table).reshape(flat_in.shape)


def norm_forward(hidden, gain_row):
    inv_rms = lax.rsqrt(jnp.mean(hidden * hidden, axis=-1, keepdims=True) + EPS)
    return ((hidden * inv_rms * gain_row.astype(jnp.float32)).astype(jnp.bfloat16), inv_rms)


def norm_reverse_pass(hidden, inv_rms, gain_row, grad_in):
    weighted = grad_in * gain_row.astype(jnp.float32)
    grad_hidden = inv_rms * weighted - hidden * (inv_rms * inv_rms * inv_rms) * jnp.mean(
        weighted * hidden, axis=-1, keepdims=True
    )
    gain_grad = jnp.sum(grad_in * hidden * inv_rms, axis=(0, 1))
    return (grad_hidden, gain_grad)


def masked_scores(query, keys, prefix_len, first_row):
    row_count = query.shape[0]
    key_count = keys.shape[0]
    kv_local = keys.shape[1] // HEAD_DIM
    grouped = query.reshape(row_count, kv_local, HEADS // KV_HEADS, HEAD_DIM)
    key_heads = keys.reshape(key_count, kv_local, HEAD_DIM)
    logits = jnp.einsum(
        "ikgd,jkd->kgij", grouped, key_heads, preferred_element_type=jnp.float32
    ) * HEAD_DIM ** (-0.5)
    query_pos = first_row + jnp.arange(row_count, dtype=jnp.int32)
    key_pos = jnp.arange(key_count, dtype=jnp.int32)
    allowed = (key_pos[None, :] <= query_pos[:, None]) | (key_pos[None, :] < prefix_len)
    return (jnp.where(allowed, logits, -1e30), grouped, key_heads)


def attend_forward(operands, first_row):
    query, keys, values, prefix_len = operands
    logits, grouped, key_heads = masked_scores(query, keys, prefix_len, first_row)
    row_max = jnp.max(logits, axis=-1, keepdims=True)
    exp_scores = jnp.exp(logits - row_max)
    row_total = jnp.sum(exp_scores, axis=-1, keepdims=True)
    probs_low = (exp_scores / row_total).astype(jnp.bfloat16)
    value_heads = values.reshape(key_heads.shape)
    mixed_out = jnp.einsum(
        "kgij,jkd->ikgd", probs_low, value_heads, preferred_element_type=jnp.float32
    )
    log_total = (row_max + jnp.log(row_total))[..., 0]
    return (mixed_out.reshape(query.shape[0], -1), log_total)


def attend_backward(operands, first_row):
    query, keys, values, prefix_len, log_total, grad_out = operands
    logits, grouped, key_heads = masked_scores(query, keys, prefix_len, first_row)
    probs = jnp.exp(logits - log_total[..., None])
    value_heads = values.reshape(key_heads.shape)
    grad_heads = grad_out.reshape(grouped.shape)
    value_grad = jnp.einsum(
        "kgij,ikgd->jkd", probs.astype(jnp.bfloat16), grad_heads, preferred_element_type=jnp.float32
    )
    grad_probs = jnp.einsum(
        "ikgd,jkd->kgij", grad_heads, value_heads, preferred_element_type=jnp.float32
    )
    delta_rows = jnp.sum(probs * grad_probs, axis=-1, keepdims=True)
    grad_scores = (probs * (grad_probs - delta_rows)).astype(jnp.bfloat16)
    query_grad = jnp.einsum(
        "kgij,jkd->ikgd", grad_scores, key_heads, preferred_element_type=jnp.float32
    ) * HEAD_DIM ** (-0.5)
    key_grad = jnp.einsum(
        "kgij,ikgd->jkd", grad_scores, grouped, preferred_element_type=jnp.float32
    ) * HEAD_DIM ** (-0.5)
    return (
        query_grad.reshape(query.shape[0], -1),
        key_grad.reshape(keys.shape[0], -1),
        value_grad.reshape(keys.shape[0], -1),
    )


def on_device(
    layer_input,
    prefix,
    attn_gain,
    q_weight,
    k_weight,
    v_weight,
    output_weight,
    mlp_gain,
    gate_weight,
    up_weight,
    down_weight,
    cotangent,
):
    row_count = layer_input.shape[1]
    key_count = row_count * lax.axis_size("context")
    first_row = lax.axis_index("context") * row_count
    cos_all, sin_all = rope_tables(key_count, HEAD_DIM)
    cos_table = lax.dynamic_slice_in_dim(cos_all, first_row, row_count, 0)
    sin_table = lax.dynamic_slice_in_dim(sin_all, first_row, row_count, 0)
    gain_one, q_full, k_full, v_full, o_full = (
        lax.all_gather(attn_gain.astype(jnp.bfloat16), ("fsdp", "context"), axis=0, tiled=True),
        lax.all_gather(q_weight.astype(jnp.bfloat16), ("fsdp", "context"), axis=0, tiled=True),
        lax.all_gather(k_weight.astype(jnp.bfloat16), ("fsdp", "context"), axis=0, tiled=True),
        lax.all_gather(v_weight.astype(jnp.bfloat16), ("fsdp", "context"), axis=0, tiled=True),
        lax.all_gather(output_weight.astype(jnp.bfloat16), ("fsdp", "context"), axis=0, tiled=True),
    )
    hidden_in = layer_input.astype(jnp.float32)
    normed_one, rms_one = norm_forward(hidden_in, gain_one)
    query = jnp.einsum("scd,de->sce", normed_one, q_full, preferred_element_type=jnp.float32)
    key_proj = jnp.einsum("scd,de->sce", normed_one, k_full, preferred_element_type=jnp.float32)
    value_low = jnp.einsum(
        "scd,de->sce", normed_one, v_full, preferred_element_type=jnp.float32
    ).astype(jnp.bfloat16)
    query_rot = rotate_rows(query, cos_table, sin_table).astype(jnp.bfloat16)
    key_rot = rotate_rows(key_proj, cos_table, sin_table).astype(jnp.bfloat16)
    keys_all, values_all = (
        lax.all_gather(key_rot, "context", axis=1, tiled=True),
        lax.all_gather(value_low, "context", axis=1, tiled=True),
    )
    attended, log_total = lax.map(
        partial(attend_forward, first_row=first_row), (query_rot, keys_all, values_all, prefix)
    )
    attended_low = attended.astype(jnp.bfloat16)
    attn_branch = lax.psum(
        jnp.einsum("sce,de->scd", attended_low, o_full, preferred_element_type=jnp.float32),
        "tensor",
    )
    resid = hidden_in + attn_branch
    gain_two, gate_full, up_full, down_full = (
        lax.all_gather(mlp_gain.astype(jnp.bfloat16), ("fsdp", "context"), axis=0, tiled=True),
        lax.all_gather(gate_weight.astype(jnp.bfloat16), ("fsdp", "context"), axis=0, tiled=True),
        lax.all_gather(up_weight.astype(jnp.bfloat16), ("fsdp", "context"), axis=0, tiled=True),
        lax.all_gather(down_weight.astype(jnp.bfloat16), ("fsdp", "context"), axis=0, tiled=True),
    )
    normed_two, rms_two = norm_forward(resid, gain_two)
    gate_proj = jnp.einsum("scd,df->scf", normed_two, gate_full, preferred_element_type=jnp.float32)
    up_projection = jnp.einsum(
        "scd,df->scf", normed_two, up_full, preferred_element_type=jnp.float32
    )
    inner_act = (jax.nn.silu(gate_proj) * up_projection).astype(jnp.bfloat16)
    mlp_branch = lax.psum(
        jnp.einsum("scf,df->scd", inner_act, down_full, preferred_element_type=jnp.float32).astype(
            jnp.bfloat16
        ),
        "tensor",
    ).astype(jnp.float32)
    layer_output = (resid + mlp_branch).astype(jnp.bfloat16)
    gain_two, gate_full, up_full, down_full = (
        lax.all_gather(mlp_gain.astype(jnp.bfloat16), ("fsdp", "context"), axis=0, tiled=True),
        lax.all_gather(gate_weight.astype(jnp.bfloat16), ("fsdp", "context"), axis=0, tiled=True),
        lax.all_gather(up_weight.astype(jnp.bfloat16), ("fsdp", "context"), axis=0, tiled=True),
        lax.all_gather(down_weight.astype(jnp.bfloat16), ("fsdp", "context"), axis=0, tiled=True),
    )
    grad_inner = jnp.einsum("scd,df->scf", cotangent, down_full, preferred_element_type=jnp.float32)
    squash = jax.nn.sigmoid(gate_proj)
    grad_gate = (grad_inner * up_projection * squash * (1.0 + gate_proj * (1.0 - squash))).astype(
        jnp.bfloat16
    )
    grad_up = (grad_inner * gate_proj * squash).astype(jnp.bfloat16)
    grad_normed_two = lax.psum(
        (
            jnp.einsum("scf,df->scd", grad_gate, gate_full, preferred_element_type=jnp.float32)
            + jnp.einsum("scf,df->scd", grad_up, up_full, preferred_element_type=jnp.float32)
        ).astype(jnp.bfloat16),
        "tensor",
    ).astype(jnp.float32)
    resid_part, gain_two_grad = norm_reverse_pass(resid, rms_two, gain_two, grad_normed_two)
    grad_resid = cotangent.astype(jnp.float32) + resid_part
    gate_part = jnp.einsum("scd,scf->df", normed_two, grad_gate, preferred_element_type=jnp.float32)
    up_part = jnp.einsum("scd,scf->df", normed_two, grad_up, preferred_element_type=jnp.float32)
    pair_part = jnp.stack([gate_part, up_part], axis=1)
    down_part = jnp.einsum("scd,scf->df", cotangent, inner_act, preferred_element_type=jnp.float32)
    mlp_grads = lax.psum_scatter(
        jnp.concatenate([pair_part, down_part[:, None, :]], axis=1),
        ("fsdp", "context"),
        scatter_dimension=0,
        tiled=True,
    )
    gate_share = mlp_grads[:, 0, :]
    up_share = mlp_grads[:, 1, :]
    down_share = mlp_grads[:, 2, :]
    gain_one, q_full, k_full, v_full, o_full = (
        lax.all_gather(attn_gain.astype(jnp.bfloat16), ("fsdp", "context"), axis=0, tiled=True),
        lax.all_gather(q_weight.astype(jnp.bfloat16), ("fsdp", "context"), axis=0, tiled=True),
        lax.all_gather(k_weight.astype(jnp.bfloat16), ("fsdp", "context"), axis=0, tiled=True),
        lax.all_gather(v_weight.astype(jnp.bfloat16), ("fsdp", "context"), axis=0, tiled=True),
        lax.all_gather(output_weight.astype(jnp.bfloat16), ("fsdp", "context"), axis=0, tiled=True),
    )
    keys_all, values_all = (
        lax.all_gather(key_rot, "context", axis=1, tiled=True),
        lax.all_gather(value_low, "context", axis=1, tiled=True),
    )
    branch_gradient = grad_resid.astype(jnp.bfloat16)
    o_part = jnp.einsum(
        "scd,sce->de", branch_gradient, attended_low, preferred_element_type=jnp.float32
    )
    grad_att = jnp.einsum(
        "scd,de->sce", branch_gradient, o_full, preferred_element_type=jnp.float32
    ).astype(jnp.bfloat16)
    query_grad, every_key_gradient, value_grad_all = lax.map(
        partial(attend_backward, first_row=first_row),
        (query_rot, keys_all, values_all, prefix, log_total, grad_att),
    )
    key_grad, value_grad = (
        lax.psum_scatter(
            every_key_gradient.astype(jnp.bfloat16), "context", scatter_dimension=1, tiled=True
        ).astype(jnp.float32),
        lax.psum_scatter(
            value_grad_all.astype(jnp.bfloat16), "context", scatter_dimension=1, tiled=True
        ).astype(jnp.float32),
    )
    query_low = rotate_rows(query_grad, cos_table, -sin_table).astype(jnp.bfloat16)
    key_low = rotate_rows(key_grad, cos_table, -sin_table).astype(jnp.bfloat16)
    value_grad_low = value_grad.astype(jnp.bfloat16)
    q_part = jnp.einsum("scd,sce->de", normed_one, query_low, preferred_element_type=jnp.float32)
    k_part = jnp.einsum("scd,sce->de", normed_one, key_low, preferred_element_type=jnp.float32)
    v_part = jnp.einsum(
        "scd,sce->de", normed_one, value_grad_low, preferred_element_type=jnp.float32
    )
    local_normed = jnp.einsum("sce,de->scd", query_low, q_full, preferred_element_type=jnp.float32)
    local_normed = local_normed + jnp.einsum(
        "sce,de->scd", key_low, k_full, preferred_element_type=jnp.float32
    )
    local_normed = local_normed + jnp.einsum(
        "sce,de->scd", value_grad_low, v_full, preferred_element_type=jnp.float32
    )
    grad_normed_one = lax.psum(local_normed.astype(jnp.bfloat16), "tensor").astype(jnp.float32)
    input_part, gain_one_grad = norm_reverse_pass(hidden_in, rms_one, gain_one, grad_normed_one)
    input_grad = (grad_resid + input_part).astype(jnp.bfloat16)
    shares = (
        lax.psum_scatter(gain_one_grad, ("fsdp", "context"), scatter_dimension=0, tiled=True),
        lax.psum_scatter(q_part, ("fsdp", "context"), scatter_dimension=0, tiled=True),
        lax.psum_scatter(k_part, ("fsdp", "context"), scatter_dimension=0, tiled=True),
        lax.psum_scatter(v_part, ("fsdp", "context"), scatter_dimension=0, tiled=True),
        lax.psum_scatter(o_part, ("fsdp", "context"), scatter_dimension=0, tiled=True),
        lax.psum_scatter(gain_two_grad, ("fsdp", "context"), scatter_dimension=0, tiled=True),
    )
    return (
        layer_output,
        input_grad,
        shares[0],
        shares[1],
        shares[2],
        shares[3],
        shares[4],
        shares[5],
        gate_share,
        up_share,
        down_share,
    )


def solution(mesh):
    placed = (
        P("fsdp", "context", None),
        P("fsdp"),
        P(("fsdp", "context")),
        P(("fsdp", "context"), "tensor"),
        P(("fsdp", "context"), "tensor"),
        P(("fsdp", "context"), "tensor"),
        P(("fsdp", "context"), "tensor"),
        P(("fsdp", "context")),
        P(("fsdp", "context"), "tensor"),
        P(("fsdp", "context"), "tensor"),
        P(("fsdp", "context"), "tensor"),
        P("fsdp", "context", None),
    )
    return jax.shard_map(
        on_device,
        mesh=mesh,
        in_specs=placed,
        out_specs=(
            P("fsdp", "context", None),
            P("fsdp", "context", None),
            P(("fsdp", "context")),
            P(("fsdp", "context"), "tensor"),
            P(("fsdp", "context"), "tensor"),
            P(("fsdp", "context"), "tensor"),
            P(("fsdp", "context"), "tensor"),
            P(("fsdp", "context")),
            P(("fsdp", "context"), "tensor"),
            P(("fsdp", "context"), "tensor"),
            P(("fsdp", "context"), "tensor"),
        ),
        check_vma=False,
    )
```

profile of v0, /device:TPU:0, one launch (start us, length us, event | category | flops | bytes accessed | tf_op | source)
XLA Modules:
  0.0 3718.7 jit_solution(15053935400837778976)
XLA Ops:
  14.9 42.2 %all-gather.2 = bf16[16,1,128]{2,1,0:T(2,128)(2,1)S(1)} all-gather(bf16[1,1,128]{2,1,0:T(2,128)(2,1)S(1)} %convert_bitcast_fusion.1), channel_id=1, replica_groups=mesh['fsdp'=4,'context'=4,'tensor'=2] {'fsdp','context'}, dimensions={0}, use_global_device_ids=true | all-gather | bytes 4352 | tf_op jit(solution)/shard_map/all_gather | solution.py:130
  71.5 55.5 %all-gather.12.cloned.1.call-done = bf16[2048,256]{1,0:T(8,128)(2,1)} async-done(((bf16[128,256]{1,0:T(8,128)(2,1)}), bf16[2048,256]{1,0:T(8,128)(2,1)}) %all-gather.12.cloned.1.call-update) | async-done | bytes 1048592 | tf_op jit(solution)/shard_map/all_gather | solution.py:133
  128.7 16.9 all-gather
  146.6 16.7 all-gather.1
  163.3 42.9 %all-gather.16.cloned.1.call-done = bf16[2048,1024]{1,0:T(8,128)(2,1)} async-done(((bf16[128,1024]{1,0:T(8,128)(2,1)}), bf16[2048,1024]{1,0:T(8,128)(2,1)}) %all-gather.16.cloned.1.call-update) | async-done | bytes 4194320 | tf_op jit(solution)/shard_map/all_gather | solution.py:131
  239.5 44.5 %all-gather.18.cloned.1.call-done = bf16[2048,1024]{1,0:T(8,128)(2,1)} async-done(((bf16[128,1024]{1,0:T(8,128)(2,1)}), bf16[2048,1024]{1,0:T(8,128)(2,1)}) %all-gather.18.cloned.1.call-update) | async-done | bytes 4194320 | tf_op jit(solution)/shard_map/all_gather | solution.py:134
  295.7 38.4 %all-gather.3 = bf16[16,1,128]{2,1,0:T(2,128)(2,1)S(1)} all-gather(bf16[1,1,128]{2,1,0:T(2,128)(2,1)S(1)} %convert_bitcast_fusion), channel_id=1, replica_groups=mesh['fsdp'=4,'context'=4,'tensor'=2] {'fsdp','context'}, dimensions={0}, use_global_device_ids=true | all-gather | bytes 4352 | tf_op jit(solution)/shard_map/all_gather | solution.py:159
  336.3 168.8 %all-gather.22.cloned.1.call-done = bf16[2048,4096]{1,0:T(8,128)(2,1)} async-done(((bf16[128,4096]{1,0:T(8,128)(2,1)}), bf16[2048,4096]{1,0:T(8,128)(2,1)}) %all-gather.22.cloned.1.call-update) | async-done | bytes 16777232 | tf_op jit(solution)/shard_map/all_gather | solution.py:161
  515.2 183.5 %all-gather.20.cloned.1.call-done = bf16[2048,4096]{1,0:T(8,128)(2,1)} async-done(((bf16[128,4096]{1,0:T(8,128)(2,1)}), bf16[2048,4096]{1,0:T(8,128)(2,1)}) %all-gather.20.cloned.1.call-update) | async-done | bytes 16777232 | tf_op jit(solution)/shard_map/all_gather | solution.py:160
  708.9 183.3 %all-gather.24.cloned.1.call-done = bf16[2048,4096]{1,0:T(8,128)(2,1)} async-done(((bf16[128,4096]{1,0:T(8,128)(2,1)}), bf16[2048,4096]{1,0:T(8,128)(2,1)}) %all-gather.24.cloned.1.call-update) | async-done | bytes 16777232 | tf_op jit(solution)/shard_map/all_gather | solution.py:162
  892.2 12.5 multiply_convert_fusion
  904.7 13.1 convolution_bitcast_fusion.1
  917.8 13.5 convolution_bitcast_fusion.2
  943.6 12.5 fusion.15
  956.2 15.4 convolution_bitcast_fusion
  990.8 15.6 fusion
  1045.8 17.5 reduce-scatter.10.cloned.1.call-done
  1066.7 66.8 %pad_maximum_fusion = f32[2048,3,4096]{2,0,1:T(8,128)} fusion(f32[2048,1,4096]{2,0,1:T(8,128)} %convolution_bitcast_fusion, f32[2048,1,4096]{2,0,1:T(8,128)} %convolution_bitcast_fusion.1, f32[2048,1,4096]{2,0,1:T(8,128)} %convolution_bitcast_fusion.2), kind=kLoop, calls=%fused_computation | loop fusion | flops 50331648 | bytes 201326592 | tf_op jit(solution)/shard_map/concatenate | solution.py:203
  1156.4 78.9 %all-reduce.2 = (f32[2048]{0:T(1024)S(1)}, f32[2048]{0:T(1024)S(1)}) all-reduce(f32[2048]{0:T(1024)S(1)} %get-tuple-element.59, f32[2048]{0:T(1024)S(1)} %get-tuple-element.57), channel_id=6, replica_groups=mesh['fsdp'=4,'context'=4,'tensor'=2] {'fsdp','context'}, use_global_device_ids=true, to_apply=%region_14.15.clone | all-reduce | flops 4096 | bytes 32768
  1240.6 1936.0 %reduce-scatter.20.cloned.1.call-done = f32[128,3,4096]{2,0,1:T(8,128)} async-done(((f32[2048,3,4096]{2,0,1:T(8,128)}), f32[128,3,4096]{2,0,1:T(8,128)}) %reduce-scatter.20.cloned.1.call-update) | async-done | bytes 6291472 | tf_op jit(solution)/shard_map/reduce_scatter | solution.py:202
  3182.4 81.5 %reduce-scatter.16.cloned.1.call-done = f32[128,256]{1,0:T(8,128)} async-done(((f32[2048,256]{1,0:T(8,128)}), f32[128,256]{1,0:T(8,128)}) %reduce-scatter.16.cloned.1.call-update) | async-done | bytes 131088 | tf_op jit(solution)/shard_map/reduce_scatter | solution.py:263
  3263.8 83.6 %reduce-scatter.14.cloned.1.call-done = f32[128,256]{1,0:T(8,128)} async-done(((f32[2048,256]{1,0:T(8,128)}), f32[128,256]{1,0:T(8,128)}) %reduce-scatter.14.cloned.1.call-update) | async-done | bytes 131088 | tf_op jit(solution)/shard_map/reduce_scatter | solution.py:262
  3347.5 181.9 %reduce-scatter.18.cloned.1.call-done = f32[128,1024]{1,0:T(8,128)} async-done(((f32[2048,1024]{1,0:T(8,128)}), f32[128,1024]{1,0:T(8,128)}) %reduce-scatter.18.cloned.1.call-update) | async-done | bytes 524304 | tf_op jit(solution)/shard_map/reduce_scatter | solution.py:264
  3529.3 182.6 %reduce-scatter.12.cloned.1.call-done = f32[128,1024]{1,0:T(8,128)} async-done(((f32[2048,1024]{1,0:T(8,128)}), f32[128,1024]{1,0:T(8,128)}) %reduce-scatter.12.cloned.1.call-update) | async-done | bytes 524304 | tf_op jit(solution)/shard_map/reduce_scatter | solution.py:261
  (196 shorter events, 198.6 us)
Async XLA Ops:
  7.2 62.3 %all-gather.14.cloned.1.call-start = ((), (), s32[]{:S(2)}) async-start(), calls=%async_computation.8 | async-start | bytes 1114112 | tf_op jit(solution)/shard_map/all_gather | solution.py:132
  8.8 118.2 %all-gather.12.cloned.1.call-start = ((), (), s32[]{:S(2)}) async-start(), calls=%async_computation.7 | async-start | bytes 1114112 | tf_op jit(solution)/shard_map/all_gather | solution.py:133
  10.4 195.8 %all-gather.16.cloned.1.call-start = ((), (), s32[]{:S(2)}) async-start(), calls=%async_computation.9 | async-start | bytes 4456448 | tf_op jit(solution)/shard_map/all_gather | solution.py:131
  12.3 271.7 %all-gather.18.cloned.1.call-start = ((), (), s32[]{:S(2)}) async-start(), calls=%async_computation.10 | async-start | bytes 4456448 | tf_op jit(solution)/shard_map/all_gather | solution.py:134
  14.1 320.0 %all-reduce.8.cloned.1.call-start = ((), (), s32[]{:S(2)}) async-start(), calls=%async_computation.11 | async-start | bytes 4194304 | tf_op jit(solution)/shard_map/psum | solution.py:153
  57.1 149.1 %copy-start.21 = (f32[16,1,128]{2,1,0:T(1,128)}, f32[16,1,128]{2,1,0:T(1,128)S(1)}, u32[]{:S(2)}) copy-start(f32[16,1,128]{2,1,0:T(1,128)S(1)} %convert_element_type.260) | copy-start | bytes 24580
  61.8 144.4 %copy-start.26 = (f32[256]{0:T(256)}, f32[256]{0:T(256)S(1)}, u32[]{:S(2)}) copy-start(f32[256]{0:T(256)S(1)} %get-tuple-element.97) | copy-start | bytes 3076
  163.3 53.2 %copy-start.7 = (bf16[1024,256]{0,1:T(8,128)(2,1)}, bf16[1024,256]{0,1:T(8,128)(2,1)S(1)}, u32[]{:S(2)}) copy-start(bf16[1024,256]{0,1:T(8,128)(2,1)S(1)} %all-gather.1) | copy-start | bytes 1572868
  239.5 44.5 %copy-start.23 = (bf16[4,64,4,256]{3,1,2,0:T(8,128)(2,1)}, bf16[4,64,4,256]{3,1,2,0:T(8,128)(2,1)S(1)}, u32[]{:S(2)}) copy-start(bf16[4,64,4,256]{3,1,2,0:T(8,128)(2,1)S(1)} %fusion.40) | copy-start | bytes 1572868
  288.8 216.4 %all-gather.22.cloned.1.call-start = ((), (), s32[]{:S(2)}) async-start(), calls=%async_computation.13 | async-start | bytes 17825792 | tf_op jit(solution)/shard_map/all_gather | solution.py:161
  291.5 407.2 %all-gather.20.cloned.1.call-start = ((), (), s32[]{:S(2)}) async-start(), calls=%async_computation.12 | async-start | bytes 17825792 | tf_op jit(solution)/shard_map/all_gather | solution.py:160
  294.4 597.8 %all-gather.24.cloned.1.call-start = ((), (), s32[]{:S(2)}) async-start(), calls=%async_computation.14 | async-start | bytes 17825792 | tf_op jit(solution)/shard_map/all_gather | solution.py:162
  295.6 688.0 %all-reduce.10.cloned.1.call-start = ((), (), s32[]{:S(2)}) async-start(), calls=%async_computation.15 | async-start | bytes 2097152 | tf_op jit(solution)/shard_map/psum | solution.py:189
  956.1 84.8 %reduce-scatter.8.cloned.1.call-start = ((), (), s32[]{:S(2)}) async-start(), calls=%async_computation.16 | async-start | bytes 655360 | tf_op jit(solution)/shard_map/reduce_scatter | solution.py:234
  990.8 15.6 slice-start.2
  990.8 15.6 slice-start.3
  1020.6 42.6 %reduce-scatter.10.cloned.1.call-start = ((), (), s32[]{:S(2)}) async-start(), calls=%async_computation.17 | async-start | bytes 655360 | tf_op jit(solution)/shard_map/reduce_scatter | solution.py:237
  1031.3 123.2 %all-reduce.12.cloned.1.call-start = ((), (), s32[]{:S(2)}) async-start(), calls=%async_computation.23 | async-start | bytes 4194304 | tf_op jit(solution)/shard_map/psum | solution.py:170
  1066.7 2109.9 %reduce-scatter.20.cloned.1.call-start = ((), (), s32[]{:S(2)}) async-start(), calls=%async_computation.22 | async-start | bytes 106954752 | tf_op jit(solution)/shard_map/reduce_scatter | solution.py:202
  1133.6 2130.2 %reduce-scatter.16.cloned.1.call-start = ((), (), s32[]{:S(2)}) async-start(), calls=%async_computation.20 | async-start | bytes 2228224 | tf_op jit(solution)/shard_map/reduce_scatter | solution.py:263
  1136.8 2210.7 %reduce-scatter.14.cloned.1.call-start = ((), (), s32[]{:S(2)}) async-start(), calls=%async_computation.19 | async-start | bytes 2228224 | tf_op jit(solution)/shard_map/reduce_scatter | solution.py:262
  1138.9 2390.5 %reduce-scatter.18.cloned.1.call-start = ((), (), s32[]{:S(2)}) async-start(), calls=%async_computation.21 | async-start | bytes 8912896 | tf_op jit(solution)/shard_map/reduce_scatter | solution.py:264
  1145.4 2566.5 %reduce-scatter.12.cloned.1.call-start = ((), (), s32[]{:S(2)}) async-start(), calls=%async_computation.18 | async-start | bytes 8912896 | tf_op jit(solution)/shard_map/reduce_scatter | solution.py:261
  1152.6 83.8 %copy-start.28 = (f32[256]{0:T(256)S(1)}, f32[256]{0:T(256)}, u32[]{:S(2)}) copy-start(f32[256]{0:T(256)} %get-tuple-element.96) | copy-start | bytes 3076
  (31 other events, 160.5 us)
Sparse Core Ops, SparseCore 0:
  11.3 58.0 all-gather.13
  72.8 54.1 all-gather.11
  130.3 75.8 all-gather.15
  209.4 74.5 all-gather.17
  288.9 19.7 all-reduce.7
  312.3 192.7 all-gather.21
  508.9 189.7 all-gather.19
  702.4 189.7 all-gather.23
  956.3 17.7 all-reduce.9
  1020.8 20.1 reduce-scatter.7
  1043.2 19.9 reduce-scatter.9
  1066.8 19.6 all-reduce.11
  1133.7 2042.8 reduce-scatter.19
  3179.3 84.4 reduce-scatter.15
  3266.5 80.8 reduce-scatter.13
  3350.2 179.1 reduce-scatter.17
  3532.1 179.8 reduce-scatter.11
where the time goes:
time: 3720 us
  waiting for transfers between devices  3170 us (85%)
  matrix products  194 us (5%)
  blocking collectives  193 us (5%)
  other arithmetic  117 us (3%)
    reduce_scatter x1, waiting for transfers between devices, on_device(): lax.psum_scatter(jnp.concatenate([pair_part, down_part[:, None, :]], axis...  1940 us
    all_gather x1, waiting for transfers between devices, on_device(): lax.all_gather(gate_weight.astype(jnp.bfloat16), ('fsdp', 'context'), axi...  183 us
    all_gather x1, waiting for transfers between devices, on_device(): lax.all_gather(down_weight.astype(jnp.bfloat16), ('fsdp', 'context'), axi...  183 us
    reduce_scatter x1, waiting for transfers between devices, on_device(): lax.psum_scatter(q_part, ('fsdp', 'context'), scatter_dimension=0, tiled=...  183 us
    reduce_scatter x1, waiting for transfers between devices, on_device(): lax.psum_scatter(o_part, ('fsdp', 'context'), scatter_dimension=0, tiled=...  182 us
    all_gather x1, waiting for transfers between devices, on_device(): lax.all_gather(up_weight.astype(jnp.bfloat16), ('fsdp', 'context'), axis=...  169 us
    reduce_scatter x1, waiting for transfers between devices, on_device(): lax.psum_scatter(k_part, ('fsdp', 'context'), scatter_dimension=0, tiled=...  83.6 us
    reduce_scatter x1, waiting for transfers between devices, on_device(): lax.psum_scatter(v_part, ('fsdp', 'context'), scatter_dimension=0, tiled=...  81.5 us
  transfers between devices with their start and end apart: 17, of which 14 were waited for; matrix products, arithmetic and copies ran while one was open for 6% of the time, Pallas kernels for 0%

commit v1 on v0

--- a/solution.py
+++ b/solution.py
@@ -9,6 +9,28 @@
 KV_HEADS = 8
 HEAD_DIM = 64
 EPS = 1e-05
+
+
+def joined_along(blocks, dim):
+    dims = list(blocks.shape[1:])
+    dims[dim] *= blocks.shape[0]
+    return jnp.moveaxis(blocks, 0, dim).reshape(dims)
+
+
+def ring_gather(x, axis, dim):
+    peers = lax.axis_size(axis)
+    pairs = [(i, (i + 1) % peers) for i in range(peers)]
+    back = [(b, a) for a, b in pairs]
+    lower, upper = ([], [])
+    for step in range(peers - 1):
+        if step % 2 == 0:
+            lower.append(lax.ppermute(lower[-1] if lower else x, axis, pairs))
+        else:
+            upper.append(lax.ppermute(upper[-1] if upper else x, axis, back))
+    pieces = jnp.stack([*lower[::-1], x, *upper])
+    shift = lax.axis_index(axis) - len(lower)
+    pieces = pieces[(jnp.arange(peers) - shift) % peers]
+    return joined_along(pieces, dim)
 
 
 def rope_tables(length, head_dim):
@@ -158,7 +180,7 @@
     gain_two, gate_full, up_full, down_full = (
         lax.all_gather(mlp_gain.astype(jnp.bfloat16), ("fsdp", "context"), axis=0, tiled=True),
         lax.all_gather(gate_weight.astype(jnp.bfloat16), ("fsdp", "context"), axis=0, tiled=True),
-        lax.all_gather(up_weight.astype(jnp.bfloat16), ("fsdp", "context"), axis=0, tiled=True),
+        ring_gather(up_weight.astype(jnp.bfloat16), ("fsdp", "context"), 0),
         lax.all_gather(down_weight.astype(jnp.bfloat16), ("fsdp", "context"), axis=0, tiled=True),
     )
     normed_two, rms_two = norm_forward(resid, gain_two)

time: 3720 us -> 3930 us (1.056)
  starting transfers between devices: 0.96 us -> 105 us
  blocking collectives: 193 us -> 262 us
    ppermute x0 -> x15, waiting for transfers between devices: none -> 411 us  [the longest x8 252 us: ring_gather(): lower.append(lax.ppermute(lower[-1] if lower else x, axis, pairs))]
    all_gather x1, waiting for transfers between devices: 183 us -> 0.01 us  [on_device(): lax.all_gather(gate_weight.astype(jnp.bfloat16), ('fsdp', 'context'), axi...]
    all_gather x1, waiting for transfers between devices: 183 us -> 0.02 us  [on_device(): lax.all_gather(down_weight.astype(jnp.bfloat16), ('fsdp', 'context'), axi...]
    ppermute x0 -> x15, starting transfers between devices: none -> 104 us  [the longest x8 84.9 us: ring_gather(): lower.append(lax.ppermute(lower[-1] if lower else x, axis, pairs))]
    all_gather x1, blocking collectives: 38.4 us -> 107 us  [on_device(): lax.all_gather(mlp_gain.astype(jnp.bfloat16), ('fsdp', 'context'), axis=0...]
    all_gather x1, waiting for transfers between devices: 169 us -> 121 us  [on_device(): lax.all_gather(up_weight.astype(jnp.bfloat16), ('fsdp', 'context'), axis=...]
  transfers between devices with their start and end apart: 17 -> 32, of which waited for: 14 -> 25; matrix products, arithmetic and copies ran while one was open for 6% -> 8% of each run, Pallas kernels for 0% -> 0%
where the time goes in v1:
time: 3930 us
  waiting for transfers between devices  3170 us (81%)
  blocking collectives  262 us (7%)
  matrix products  196 us (5%)
  other arithmetic  122 us (3%)
  starting transfers between devices  105 us (3%)
  local copies, waits for them, and re-layouts  60.5 us (2%)
    reduce_scatter x1, waiting for transfers between devices, on_device(): lax.psum_scatter(jnp.concatenate([pair_part, down_part[:, None, :]], axis...  1940 us
    ppermute x8, waiting for transfers between devices, ring_gather(): lower.append(lax.ppermute(lower[-1] if lower else x, axis, pairs))  252 us
    reduce_scatter x1, waiting for transfers between devices, on_device(): lax.psum_scatter(q_part, ('fsdp', 'context'), scatter_dimension=0, tiled=...  183 us
    reduce_scatter x1, waiting for transfers between devices, on_device(): lax.psum_scatter(o_part, ('fsdp', 'context'), scatter_dimension=0, tiled=...  182 us
    ppermute x7, waiting for transfers between devices, ring_gather(): upper.append(lax.ppermute(upper[-1] if upper else x, axis, back))  159 us
    all_gather x1, waiting for transfers between devices, on_device(): lax.all_gather(up_weight.astype(jnp.bfloat16), ('fsdp', 'context'), axis=...  121 us
    all_gather x1, blocking collectives, on_device(): lax.all_gather(mlp_gain.astype(jnp.bfloat16), ('fsdp', 'context'), axis=0...  107 us
    ppermute x8, starting transfers between devices, ring_gather(): lower.append(lax.ppermute(lower[-1] if lower else x, axis, pairs))  84.9 us
  transfers between devices with their start and end apart: 32, of which 25 were waited for; matrix products, arithmetic and copies ran while one was open for 8% of the time, Pallas kernels for 0%

profile of v1, /device:TPU:0, one launch (start us, length us, event | category | flops | bytes accessed | tf_op | source)
XLA Modules:
  0.0 3927.1 jit_solution(6090260077784476551)
XLA Ops:
  15.6 42.2 %all-gather.2 = bf16[16,1,128]{2,1,0:T(2,128)(2,1)S(1)} all-gather(bf16[1,1,128]{2,1,0:T(2,128)(2,1)S(1)} %convert_bitcast_fusion.1), channel_id=1, replica_groups=mesh['fsdp'=4,'context'=4,'tensor'=2] {'fsdp','context'}, dimensions={0}, use_global_device_ids=true | all-gather | bytes 4352 | tf_op jit(solution)/shard_map/all_gather | solution.py:152
  71.4 55.5 %all-gather.12.cloned.1.call-done = bf16[2048,256]{1,0:T(8,128)(2,1)} async-done(((bf16[128,256]{1,0:T(8,128)(2,1)}), bf16[2048,256]{1,0:T(8,128)(2,1)}) %all-gather.12.cloned.1.call-update) | async-done | bytes 1048592 | tf_op jit(solution)/shard_map/all_gather | solution.py:155
  163.5 42.7 %all-gather.16.cloned.1.call-done = bf16[2048,1024]{1,0:T(8,128)(2,1)} async-done(((bf16[128,1024]{1,0:T(8,128)(2,1)}), bf16[2048,1024]{1,0:T(8,128)(2,1)}) %all-gather.16.cloned.1.call-update) | async-done | bytes 4194320 | tf_op jit(solution)/shard_map/all_gather | solution.py:153
  239.6 44.4 %all-gather.18.cloned.1.call-done = bf16[2048,1024]{1,0:T(8,128)(2,1)} async-done(((bf16[128,1024]{1,0:T(8,128)(2,1)}), bf16[2048,1024]{1,0:T(8,128)(2,1)}) %all-gather.18.cloned.1.call-update) | async-done | bytes 4194320 | tf_op jit(solution)/shard_map/all_gather | solution.py:156
  328.9 45.8 %collective-permute-done.1 = bf16[128,4096]{1,0:T(8,128)(2,1)S(1)} collective-permute-done((bf16[128,4096]{1,0:T(8,128)(2,1)}, bf16[128,4096]{1,0:T(8,128)(2,1)S(1)}, u32[]{:S(2)}, u32[]{:S(2)}) %collective-permute-start.1) | collective-permute-done | bytes 1048608 | tf_op jit(solution)/shard_map/ppermute | solution.py:27
  374.7 33.9 collective-permute-done.8
  409.5 38.0 collective-permute-done.2
  447.5 26.4 collective-permute-start.3
  487.2 42.2 %collective-permute-done.3 = bf16[128,4096]{1,0:T(8,128)(2,1)S(1)} collective-permute-done((bf16[128,4096]{1,0:T(8,128)(2,1)S(1)}, bf16[128,4096]{1,0:T(8,128)(2,1)S(1)}, u32[]{:S(2)}, u32[]{:S(2)}) %collective-permute-start.3) | collective-permute-done | bytes 1048608 | tf_op jit(solution)/shard_map/ppermute | solution.py:27
  529.4 27.2 collective-permute-start.4
  576.2 43.1 %collective-permute-done.4 = bf16[128,4096]{1,0:T(8,128)(2,1)S(1)} collective-permute-done((bf16[128,4096]{1,0:T(8,128)(2,1)S(1)}, bf16[128,4096]{1,0:T(8,128)(2,1)S(1)}, u32[]{:S(2)}, u32[]{:S(2)}) %collective-permute-start.4) | collective-permute-done | bytes 1048608 | tf_op jit(solution)/shard_map/ppermute | solution.py:27
  619.3 29.8 collective-permute-start.5
  692.4 40.0 %collective-permute-done.12 = bf16[128,4096]{1,0:T(8,128)(2,1)} collective-permute-done((bf16[128,4096]{1,0:T(8,128)(2,1)S(1)}, bf16[128,4096]{1,0:T(8,128)(2,1)}, u32[]{:S(2)}, u32[]{:S(2)}) %collective-permute-start.12) | collective-permute-done | bytes 1048608 | tf_op jit(solution)/shard_map/ppermute | solution.py:29
  734.6 30.9 collective-permute-done.6
  765.5 107.1 %all-gather.3 = bf16[16,1,128]{2,1,0:T(2,128)(2,1)S(1)} all-gather(bf16[1,1,128]{2,1,0:T(2,128)(2,1)S(1)} %convert_bitcast_fusion), channel_id=1, replica_groups=mesh['fsdp'=4,'context'=4,'tensor'=2] {'fsdp','context'}, dimensions={0}, use_global_device_ids=true | all-gather | bytes 4352 | tf_op jit(solution)/shard_map/all_gather | solution.py:181
  900.9 42.4 %collective-permute-done.14 = bf16[128,4096]{1,0:T(8,128)(2,1)S(1)} collective-permute-done((bf16[128,4096]{1,0:T(8,128)(2,1)}, bf16[128,4096]{1,0:T(8,128)(2,1)S(1)}, u32[]{:S(2)}, u32[]{:S(2)}) %collective-permute-start.14) | collective-permute-done | bytes 1048608 | tf_op jit(solution)/shard_map/ppermute | solution.py:29
  1031.5 120.7 %all-gather.24.cloned.1.call-done = bf16[2048,4096]{1,0:T(8,128)(2,1)} async-done(((bf16[128,4096]{1,0:T(8,128)(2,1)}), bf16[2048,4096]{1,0:T(8,128)(2,1)}) %all-gather.24.cloned.1.call-update) | async-done | bytes 16777232 | tf_op jit(solution)/shard_map/all_gather | solution.py:202
  1275.8 66.8 %pad_maximum_fusion = f32[2048,3,4096]{2,0,1:T(8,128)} fusion(f32[2048,1,4096]{2,0,1:T(8,128)} %convolution_bitcast_fusion, f32[2048,1,4096]{2,0,1:T(8,128)} %convolution_bitcast_fusion.1, f32[2048,1,4096]{2,0,1:T(8,128)} %convolution_bitcast_fusion.2), kind=kLoop, calls=%fused_computation.1 | loop fusion | flops 50331648 | bytes 201326592 | tf_op jit(solution)/shard_map/concatenate | solution.py:225
  1365.3 79.0 %all-reduce.2 = (f32[2048]{0:T(1024)S(1)}, f32[2048]{0:T(1024)S(1)}) all-reduce(f32[2048]{0:T(1024)S(1)} %get-tuple-element.59, f32[2048]{0:T(1024)S(1)} %get-tuple-element.57), channel_id=6, replica_groups=mesh['fsdp'=4,'context'=4,'tensor'=2] {'fsdp','context'}, use_global_device_ids=true, to_apply=%region_14.15.clone | all-reduce | flops 4096 | bytes 32768
  1449.6 1935.5 %reduce-scatter.20.cloned.1.call-done = f32[128,3,4096]{2,0,1:T(8,128)} async-done(((f32[2048,3,4096]{2,0,1:T(8,128)}), f32[128,3,4096]{2,0,1:T(8,128)}) %reduce-scatter.20.cloned.1.call-update) | async-done | bytes 6291472 | tf_op jit(solution)/shard_map/reduce_scatter | solution.py:224
  3390.9 81.7 %reduce-scatter.16.cloned.1.call-done = f32[128,256]{1,0:T(8,128)} async-done(((f32[2048,256]{1,0:T(8,128)}), f32[128,256]{1,0:T(8,128)}) %reduce-scatter.16.cloned.1.call-update) | async-done | bytes 131088 | tf_op jit(solution)/shard_map/reduce_scatter | solution.py:285
  3472.6 83.7 %reduce-scatter.14.cloned.1.call-done = f32[128,256]{1,0:T(8,128)} async-done(((f32[2048,256]{1,0:T(8,128)}), f32[128,256]{1,0:T(8,128)}) %reduce-scatter.14.cloned.1.call-update) | async-done | bytes 131088 | tf_op jit(solution)/shard_map/reduce_scatter | solution.py:284
  3556.2 181.6 %reduce-scatter.18.cloned.1.call-done = f32[128,1024]{1,0:T(8,128)} async-done(((f32[2048,1024]{1,0:T(8,128)}), f32[128,1024]{1,0:T(8,128)}) %reduce-scatter.18.cloned.1.call-update) | async-done | bytes 524304 | tf_op jit(solution)/shard_map/reduce_scatter | solution.py:286
  3737.8 182.6 %reduce-scatter.12.cloned.1.call-done = f32[128,1024]{1,0:T(8,128)} async-done(((f32[2048,1024]{1,0:T(8,128)}), f32[128,1024]{1,0:T(8,128)}) %reduce-scatter.12.cloned.1.call-update) | async-done | bytes 524304 | tf_op jit(solution)/shard_map/reduce_scatter | solution.py:283
  (273 shorter events, 488.0 us)
Async XLA Ops:
  8.8 118.2 %all-gather.12.cloned.1.call-start = ((), (), s32[]{:S(2)}) async-start(), calls=%async_computation.7 | async-start | bytes 1114112 | tf_op jit(solution)/shard_map/all_gather | solution.py:155
  10.4 195.9 %all-gather.16.cloned.1.call-start = ((), (), s32[]{:S(2)}) async-start(), calls=%async_computation.9 | async-start | bytes 4456448 | tf_op jit(solution)/shard_map/all_gather | solution.py:153
  12.3 271.7 %all-gather.18.cloned.1.call-start = ((), (), s32[]{:S(2)}) async-start(), calls=%async_computation.10 | async-start | bytes 4456448 | tf_op jit(solution)/shard_map/all_gather | solution.py:156
  14.2 943.8 %all-reduce.8.cloned.1.call-start = ((), (), s32[]{:S(2)}) async-start(), calls=%async_computation.11 | async-start | bytes 4194304 | tf_op jit(solution)/shard_map/psum | solution.py:175
  288.8 671.4 %all-gather.22.cloned.1.call-start = ((), (), s32[]{:S(2)}) async-start(), calls=%async_computation.13 | async-start | bytes 17825792 | tf_op jit(solution)/shard_map/all_gather | solution.py:184
  291.8 681.1 %all-gather.20.cloned.1.call-start = ((), (), s32[]{:S(2)}) async-start(), calls=%async_computation.12 | async-start | bytes 17825792 | tf_op jit(solution)/shard_map/all_gather | solution.py:182
  294.5 857.7 %all-gather.24.cloned.1.call-start = ((), (), s32[]{:S(2)}) async-start(), calls=%async_computation.14 | async-start | bytes 17825792 | tf_op jit(solution)/shard_map/all_gather | solution.py:202
  297.2 895.1 %all-reduce.10.cloned.1.call-start = ((), (), s32[]{:S(2)}) async-start(), calls=%async_computation.15 | async-start | bytes 2097152 | tf_op jit(solution)/shard_map/psum | solution.py:211
  323.3 85.2 %collective-permute-start.8 = (bf16[128,4096]{1,0:T(8,128)(2,1)}, bf16[128,4096]{1,0:T(8,128)(2,1)S(1)}, u32[]{:S(2)}, u32[]{:S(2)}) collective-permute-start(bf16[128,4096]{1,0:T(8,128)(2,1)} %convert_element_type.228), channel_id=1, source_target_pairs={{2,0},{4,2},{6,4},{8,6},{10,8},{12,10},{14,12},{16,14},{18,16},{20... | collective-permute-start | bytes 3145736 | tf_op jit(solution)/shard_map/ppermute | solution.py:29
  447.5 81.9 %collective-permute-start.3 = (bf16[128,4096]{1,0:T(8,128)(2,1)S(1)}, bf16[128,4096]{1,0:T(8,128)(2,1)S(1)}, u32[]{:S(2)}, u32[]{:S(2)}) collective-permute-start(bf16[128,4096]{1,0:T(8,128)(2,1)S(1)} %collective-permute-done.2), channel_id=1, source_target_pairs={{0,2},{2,4},{4,6},{6,8},{8,10},{10,12},{12,14},{14,16},{16,18},{18... | collective-permute-start | bytes 3145736 | tf_op jit(solution)/shard_map/ppermute | solution.py:27
  481.5 93.7 %collective-permute-start.10 = (bf16[128,4096]{1,0:T(8,128)(2,1)S(1)}, bf16[128,4096]{1,0:T(8,128)(2,1)S(1)}, u32[]{:S(2)}, u32[]{:S(2)}) collective-permute-start(bf16[128,4096]{1,0:T(8,128)(2,1)S(1)} %collective-permute-done.9), channel_id=1, source_target_pairs={{2,0},{4,2},{6,4},{8,6},{10,8},{12,10},{14,12},{16,14},{18,16},{20... | collective-permute-start | bytes 3145736 | tf_op jit(solution)/shard_map/ppermute | solution.py:29
  529.4 89.9 %collective-permute-start.4 = (bf16[128,4096]{1,0:T(8,128)(2,1)S(1)}, bf16[128,4096]{1,0:T(8,128)(2,1)S(1)}, u32[]{:S(2)}, u32[]{:S(2)}) collective-permute-start(bf16[128,4096]{1,0:T(8,128)(2,1)S(1)} %collective-permute-done.3), channel_id=1, source_target_pairs={{0,2},{2,4},{4,6},{6,8},{8,10},{10,12},{12,14},{14,16},{16,18},{18... | collective-permute-start | bytes 3145736 | tf_op jit(solution)/shard_map/ppermute | solution.py:27
  575.2 90.3 %collective-permute-start.11 = (bf16[128,4096]{1,0:T(8,128)(2,1)S(1)}, bf16[128,4096]{1,0:T(8,128)(2,1)S(1)}, u32[]{:S(2)}, u32[]{:S(2)}) collective-permute-start(bf16[128,4096]{1,0:T(8,128)(2,1)S(1)} %collective-permute-done.10), channel_id=1, source_target_pairs={{2,0},{4,2},{6,4},{8,6},{10,8},{12,10},{14,12},{16,14},{18,16},{20... | collective-permute-start | bytes 3145736 | tf_op jit(solution)/shard_map/ppermute | solution.py:29
  619.3 73.1 %collective-permute-start.5 = (bf16[128,4096]{1,0:T(8,128)(2,1)S(1)}, bf16[128,4096]{1,0:T(8,128)(2,1)S(1)}, u32[]{:S(2)}, u32[]{:S(2)}) collective-permute-start(bf16[128,4096]{1,0:T(8,128)(2,1)S(1)} %collective-permute-done.4), channel_id=1, source_target_pairs={{0,2},{2,4},{4,6},{6,8},{8,10},{10,12},{12,14},{14,16},{16,18},{18... | collective-permute-start | bytes 3145736 | tf_op jit(solution)/shard_map/ppermute | solution.py:27
  692.4 73.1 %collective-permute-start.6 = (bf16[128,4096]{1,0:T(8,128)(2,1)S(1)}, bf16[128,4096]{1,0:T(8,128)(2,1)}, u32[]{:S(2)}, u32[]{:S(2)}) collective-permute-start(bf16[128,4096]{1,0:T(8,128)(2,1)S(1)} %collective-permute-done.5), channel_id=1, source_target_pairs={{0,2},{2,4},{4,6},{6,8},{8,10},{10,12},{12,14},{14,16},{16,18},{18... | collective-permute-start | bytes 3145736 | tf_op jit(solution)/shard_map/ppermute | solution.py:27
  732.4 140.2 %collective-permute-start.13 = (bf16[128,4096]{1,0:T(8,128)(2,1)}, bf16[128,4096]{1,0:T(8,128)(2,1)}, u32[]{:S(2)}, u32[]{:S(2)}) collective-permute-start(bf16[128,4096]{1,0:T(8,128)(2,1)} %collective-permute-done.12), channel_id=1, source_target_pairs={{2,0},{4,2},{6,4},{8,6},{10,8},{12,10},{14,12},{16,14},{18,16},{20... | collective-permute-start | bytes 3145736 | tf_op jit(solution)/shard_map/ppermute | solution.py:29
  765.5 112.7 %collective-permute-start.7 = (bf16[128,4096]{1,0:T(8,128)(2,1)}, bf16[128,4096]{1,0:T(8,128)(2,1)}, u32[]{:S(2)}, u32[]{:S(2)}) collective-permute-start(bf16[128,4096]{1,0:T(8,128)(2,1)} %collective-permute-done.6), channel_id=1, source_target_pairs={{0,2},{2,4},{4,6},{6,8},{8,10},{10,12},{12,14},{14,16},{16,18},{18... | collective-permute-start | bytes 3145736 | tf_op jit(solution)/shard_map/ppermute | solution.py:27
  1164.8 85.4 %reduce-scatter.8.cloned.1.call-start = ((), (), s32[]{:S(2)}) async-start(), calls=%async_computation.16 | async-start | bytes 655360 | tf_op jit(solution)/shard_map/reduce_scatter | solution.py:256
  1240.5 122.9 %all-reduce.12.cloned.1.call-start = ((), (), s32[]{:S(2)}) async-start(), calls=%async_computation.23 | async-start | bytes 4194304 | tf_op jit(solution)/shard_map/psum | solution.py:192
  1275.7 2109.4 %reduce-scatter.20.cloned.1.call-start = ((), (), s32[]{:S(2)}) async-start(), calls=%async_computation.22 | async-start | bytes 106954752 | tf_op jit(solution)/shard_map/reduce_scatter | solution.py:224
  1342.7 2129.9 %reduce-scatter.16.cloned.1.call-start = ((), (), s32[]{:S(2)}) async-start(), calls=%async_computation.20 | async-start | bytes 2228224 | tf_op jit(solution)/shard_map/reduce_scatter | solution.py:285
  1345.8 2210.5 %reduce-scatter.14.cloned.1.call-start = ((), (), s32[]{:S(2)}) async-start(), calls=%async_computation.19 | async-start | bytes 2228224 | tf_op jit(solution)/shard_map/reduce_scatter | solution.py:284
  1347.8 2390.0 %reduce-scatter.18.cloned.1.call-start = ((), (), s32[]{:S(2)}) async-start(), calls=%async_computation.21 | async-start | bytes 8912896 | tf_op jit(solution)/shard_map/reduce_scatter | solution.py:286
  1354.2 2566.1 %reduce-scatter.12.cloned.1.call-start = ((), (), s32[]{:S(2)}) async-start(), calls=%async_computation.18 | async-start | bytes 8912896 | tf_op jit(solution)/shard_map/reduce_scatter | solution.py:283
  (60 other events, 2484.6 us)
Sparse Core Ops, SparseCore 0:
  11.3 58.0 all-gather.13
  72.8 54.1 all-gather.11
  130.3 75.9 all-gather.15
  209.4 74.4 all-gather.17
  288.9 19.7 all-reduce.7
  312.3 355.1 all-gather.21
  671.2 285.3 all-gather.19
  959.7 192.5 all-gather.23
  1164.9 17.7 all-reduce.9
  1229.9 20.1 reduce-scatter.7
  1252.4 19.8 reduce-scatter.9
  1275.9 19.5 all-reduce.11
  1342.8 2042.2 reduce-scatter.19
  3387.8 84.7 reduce-scatter.15
  3475.3 80.9 reduce-scatter.13
  3559.0 178.7 reduce-scatter.17
  3740.5 179.8 reduce-scatter.11
